TPU v7x, 128 devices: a whole 4x4x4 slice. The times are simulated.
128 devices in a mesh: row: 16 (over y, z), col: 8 (over x, core).
Axes of the slice: x: 4, y: 4, z: 4, core: 2. Of those that a mesh axis runs over, the one named last changes fastest.
Arguments:
- tokens: bfloat16 [2048, 4096], P('row', 'col'), may hold values from -6 to 6
- w_in: bfloat16 [4096, 16384], P('col', 'row'), may hold values from -0.09375 to 0.09375
- w_out: bfloat16 [16384, 4096], P('row', 'col'), may hold values from -0.046875 to 0.046875
- cotangent: bfloat16 [2048, 4096], P('row', 'col'), may hold values from -6 to 6
Outputs:
- block_out: bfloat16 [2048, 4096], P(('row', 'col'))
- grad_tokens: bfloat16 [2048, 4096], P('row', 'col')
- grad_in: float32 [4096, 16384], P('col', 'row')
- grad_out: float32 [16384, 4096], P('row', 'col')
All inputs are finite; a program needn't handle non-finite values.
Results may differ from a plain program's by a relative error of at most 0.015.
Values may be sent and summed in bfloat16 or wider, within the bound.
A program may use at most 128 MiB of HBM per device.

v0:
```python
import jax
import jax.numpy as jnp
from jax import lax
from jax.sharding import PartitionSpec as P


def gelu_grad(value):
    cdf = 0.5 * (1.0 + jax.scipy.special.erf(value * 0.7071067811865476))
    pdf = jnp.exp(-0.5 * value * value) * 0.3989422804014327
    return cdf + value * pdf


def token_panel(local_rows):
    return lax.all_gather(local_rows, "row", axis=0, tiled=True)


def token_panel_a2a(local_rows):
    n = lax.axis_size("row")
    copies = jnp.broadcast_to(local_rows[None], (n,) + local_rows.shape)
    copies = copies.reshape(n * local_rows.shape[0], local_rows.shape[1])
    return lax.all_to_all(copies, "row", split_axis=0, concat_axis=0, tiled=True)


def hidden_panel(local_rows):
    return lax.all_gather(local_rows, "col", axis=0, tiled=True)


def contract_last(left, right):
    return lax.dot_general(
        left, right, (((1,), (1,)), ((), ())), preferred_element_type=jnp.float32
    )


def width_split(left_all, right, transposed):
    if transposed:
        term = contract_last(left_all, right)
    else:
        term = jnp.dot(left_all, right, preferred_element_type=jnp.float32)
    return lax.psum_scatter(
        term.astype(jnp.bfloat16), "col", scatter_dimension=0, tiled=True
    ).astype(jnp.float32)


def unit_sum(left_all, right, transposed):
    n = lax.axis_size("row")
    if transposed:
        term = contract_last(left_all, right)
    else:
        term = jnp.dot(left_all, right, preferred_element_type=jnp.float32)
    pieces = term.astype(jnp.bfloat16).reshape(n, term.shape[0] // n, term.shape[1])
    pieces = lax.all_to_all(pieces, "row", split_axis=0, concat_axis=0, tiled=True)
    return jnp.sum(pieces.astype(jnp.float32), axis=0)


def local(tokens, w_in, w_out, cotangent):
    tokens_all = token_panel(tokens)
    upstream_all = token_panel_a2a(cotangent)
    pre_part = width_split(tokens_all, w_in, False)
    act_all = hidden_panel(jax.nn.gelu(pre_part, approximate=False).astype(jnp.bfloat16))
    dact_part = width_split(upstream_all, w_out, True)
    dpre_all = hidden_panel((dact_part * gelu_grad(pre_part)).astype(jnp.bfloat16))
    mixed = unit_sum(act_all, w_out, False)
    block_rows = (tokens.astype(jnp.float32) + mixed).astype(jnp.bfloat16)
    block_out = lax.all_to_all(block_rows, "col", split_axis=0, concat_axis=1, tiled=True)
    grad_out = lax.dot_general(
        act_all, upstream_all, (((0,), (0,)), ((), ())), preferred_element_type=jnp.float32
    )
    grad_in = lax.dot_general(
        tokens_all, dpre_all, (((0,), (0,)), ((), ())), preferred_element_type=jnp.float32
    )
    back = unit_sum(dpre_all, w_in, True)
    grad_tokens = (cotangent.astype(jnp.float32) + back).astype(jnp.bfloat16)
    return (block_out, grad_tokens, grad_in, grad_out)


def solution(mesh):
    in_specs = (P("row", "col"), P("col", "row"), P("row", "col"), P("row", "col"))
    out_specs = (P(("row", "col"), None), P("row", "col"), P("col", "row"), P("row", "col"))
    return jax.shard_map(local, mesh=mesh, in_specs=in_specs, out_specs=out_specs, check_vma=False)
```

profile of v0, /device:TPU:1, one launch (start us, length us, event | category | flops | bytes accessed | tf_op | source)
XLA Modules:
  0.0 260.2 jit_solution(16874489885100301524)
XLA Ops:
  8.1 0.7 all-gather.4.cloned.1.call-update
  8.8 1.1 broadcast_in_dim.2
  9.9 37.6 %all_to_all.38 = bf16[16,128,512]{2,1,0:T(8,128)(2,1)S(1)} all-to-all(bf16[16,128,512]{2,1,0:T(8,128)(2,1)S(1)} %broadcast_in_dim.2), channel_id=1, replica_groups=mesh['row'=16,'col'=8] {'row'}, dimensions={0} | all-to-all | bytes 4194304 | tf_op jit(solution)/shard_map/all_to_all | solution.py:21
  47.5 1.4 copy-done.1
  48.9 4.3 %convolution_convert_fusion = bf16[2048,1024]{1,0:T(8,128)(2,1)} fusion(bf16[2048,512]{1,0:T(8,128)(2,1)S(1)} %bitcast.21, bf16[1024,512]{1,0:T(8,128)(2,1)S(1)} %copy-done), kind=kOutput, calls=%fused_computation.2 | convolution fusion | flops 2149580800 | bytes 7340032 | tf_op jit(solution)/shard_map/dot_general | solution.py:29
  53.3 0.0 reduce-scatter.3.cloned.1.call-start
  53.3 12.5 %all-gather.4.cloned.1.call-done = bf16[2048,512]{1,0:T(8,128)(2,1)} async-done(((bf16[128,512]{1,0:T(8,128)(2,1)}), bf16[2048,512]{1,0:T(8,128)(2,1)}) %all-gather.4.cloned.1.call-update) | async-done | bytes 2097168 | tf_op jit(solution)/shard_map/all_gather | solution.py:14
  65.8 5.9 %convolution_convert_fusion.1 = bf16[2048,1024]{1,0:T(8,128)(2,1)} fusion(bf16[2048,512]{1,0:T(8,128)(2,1)} %all-gather.4.cloned.1.call-done, bf16[512,1024]{1,0:T(8,128)(2,1)S(1)} %copy-done.4), kind=kOutput, calls=%fused_computation.3 | convolution fusion | flops 2149580800 | bytes 7340032 | tf_op jit(solution)/shard_map/dot_general | solution.py:38
  71.8 0.0 all-gather.6.cloned.1.call-start
  71.9 15.8 %reduce-scatter.5.cloned.1.call-done = bf16[256,1024]{1,0:T(8,128)(2,1)} async-done(((bf16[2048,1024]{1,0:T(8,128)(2,1)}), bf16[256,1024]{1,0:T(8,128)(2,1)}) %reduce-scatter.5.cloned.1.call-update) | async-done | bytes 524304 | tf_op jit(solution)/shard_map/reduce_scatter | solution.py:39
  87.7 38.8 %reduce-scatter.3.cloned.1.call-done = bf16[256,1024]{1,0:T(8,128)(2,1)} async-done(((bf16[2048,1024]{1,0:T(8,128)(2,1)}), bf16[256,1024]{1,0:T(8,128)(2,1)}) %reduce-scatter.3.cloned.1.call-update) | async-done | bytes 524304 | tf_op jit(solution)/shard_map/reduce_scatter | solution.py:39
  126.4 4.6 %fusion.38 = (bf16[256,1024]{1,0:T(8,128)(2,1)}, bf16[256,1024]{1,0:T(8,128)(2,1)}) fusion(bf16[256,1024]{1,0:T(8,128)(2,1)} %reduce-scatter.3.cloned.1.call-done, bf16[256,1024]{1,0:T(8,128)(2,1)} %reduce-scatter.5.cloned.1.call-done), kind=kLoop, calls=%fused_computation.52 | loop fusion | flops 20185088 | bytes 2097152 | tf_op jit(solution)/shard_map/convert_element_type | solution.py:61
  131.1 0.7 all-gather.8.cloned.1.call-update
  131.8 33.5 %all-gather.6.cloned.1.call-done = bf16[2048,1024]{1,0:T(8,128)(2,1)} async-done(((bf16[256,1024]{1,0:T(8,128)(2,1)}), bf16[2048,1024]{1,0:T(8,128)(2,1)}) %all-gather.6.cloned.1.call-update) | async-done | bytes 4194320 | tf_op jit(solution)/shard_map/all_gather | solution.py:25
  165.3 5.8 %convolution_convert_fusion.3 = bf16[2048,512]{1,0:T(8,128)(2,1)} fusion(bf16[2048,1024]{1,0:T(8,128)(2,1)} %all-gather.6.cloned.1.call-done, bf16[1024,512]{1,0:T(8,128)(2,1)S(1)} %copy-done), kind=kOutput, calls=%fused_computation.5 | convolution fusion | flops 2148532224 | bytes 7340032 | tf_op jit(solution)/shard_map/dot_general | solution.py:49
  171.1 6.7 %all-to-all-start = ((bf16[16,128,512]{2,1,0:T(8,128)(2,1)}), bf16[16,128,512]{2,1,0:T(8,128)(2,1)S(1)}, u32[]{:S(2)}, u32[]{:S(2)}) async-start(bf16[16,128,512]{2,1,0:T(8,128)(2,1)} %bitcast.24), calls=%async_computation.1 | async-start | bytes 4194304 | tf_op jit(solution)/shard_map/all_to_all | solution.py:51
  177.9 21.7 %all-gather.8.cloned.1.call-done = bf16[2048,1024]{1,0:T(8,128)(2,1)} async-done(((bf16[256,1024]{1,0:T(8,128)(2,1)}), bf16[2048,1024]{1,0:T(8,128)(2,1)}) %all-gather.8.cloned.1.call-update) | async-done | bytes 4194320 | tf_op jit(solution)/shard_map/all_gather | solution.py:25
  199.5 6.2 %convolution_convert_fusion.2 = bf16[2048,512]{1,0:T(8,128)(2,1)} fusion(bf16[2048,1024]{1,0:T(8,128)(2,1)} %all-gather.8.cloned.1.call-done, bf16[512,1024]{1,0:T(8,128)(2,1)} %param.5), kind=kOutput, calls=%fused_computation.4 | convolution fusion | flops 2148532224 | bytes 7340032 | tf_op jit(solution)/shard_map/dot_general | solution.py:29
  205.7 1.4 all-to-all-done
  207.1 5.4 %all-to-all-start.3 = ((bf16[16,128,512]{2,1,0:T(8,128)(2,1)}), bf16[16,128,512]{2,1,0:T(8,128)(2,1)}, u32[]{:S(2)}, u32[]{:S(2)}) async-start(bf16[16,128,512]{2,1,0:T(8,128)(2,1)} %bitcast.23), calls=%async_computation.5 | async-start | bytes 4194304 | tf_op jit(solution)/shard_map/all_to_all | solution.py:51
  212.5 6.6 %convolution_bitcast_fusion = f32[512,1024]{0,1:T(8,128)} fusion(bf16[2048,1024]{1,0:T(8,128)(2,1)} %all-gather.8.cloned.1.call-done, bf16[2048,512]{1,0:T(8,128)(2,1)} %all-gather.4.cloned.1.call-done), kind=kOutput, calls=%fused_computation.12 | convolution fusion | flops 2147483648 | bytes 8388608 | tf_op jit(solution)/shard_map/dot_general | solution.py:68
  219.0 2.9 %copy.12 = f32[512,1024]{1,0:T(8,128)} copy(f32[512,1024]{0,1:T(8,128)} %convolution_bitcast_fusion) | data formatting | bytes 4194304
  221.9 6.5 %fusion.39 = f32[1024,512]{1,0:T(8,128)} fusion(bf16[2048,1024]{1,0:T(8,128)(2,1)} %all-gather.6.cloned.1.call-done, bf16[2048,512]{1,0:T(8,128)(2,1)} %bitcast.22), kind=kOutput, calls=%fused_computation.55 | convolution fusion | flops 2147483648 | bytes 8388608 | tf_op jit(solution)/shard_map/dot_general | solution.py:65
  228.5 0.3 convert_reduce_fusion.1
  228.8 0.6 copy-done.3
  229.4 0.7 add_convert_fusion.1
  230.0 8.0 %all-to-all-done.3 = bf16[16,128,512]{2,1,0:T(8,128)(2,1)} async-done(((bf16[16,128,512]{2,1,0:T(8,128)(2,1)}), bf16[16,128,512]{2,1,0:T(8,128)(2,1)}, u32[]{:S(2)}, u32[]{:S(2)}) %all-to-all-start.3) | async-done | bytes 2097184 | tf_op jit(solution)/shard_map/all_to_all | solution.py:51
  238.1 8.6 %all-to-all-start.1 = ((bf16[8,16,512]{2,1,0:T(8,128)(2,1)}), bf16[8,16,512]{2,1,0:T(8,128)(2,1)S(1)}, u32[]{:S(2)}, u32[]{:S(2)}) async-start(bf16[8,16,512]{2,1,0:T(8,128)(2,1)} %bitcast.1), calls=%async_computation.2 | async-start | bytes 262144 | tf_op jit(solution)/shard_map/all_to_all | solution.py:64
  246.7 1.9 convert_reduce_fusion
  248.6 0.7 add_convert_fusion
  249.3 2.7 %all-to-all-done.1 = bf16[8,16,512]{2,1,0:T(8,128)(2,1)S(1)} async-done(((bf16[8,16,512]{2,1,0:T(8,128)(2,1)}), bf16[8,16,512]{2,1,0:T(8,128)(2,1)S(1)}, u32[]{:S(2)}, u32[]{:S(2)}) %all-to-all-start.1) | async-done | bytes 131104 | tf_op jit(solution)/shard_map/all_to_all | solution.py:64
  252.0 0.7 copy.13
  (14 shorter events, 0.2 us)
Async XLA Ops:
  8.0 40.9 %copy-start = (bf16[1024,512]{1,0:T(8,128)(2,1)S(1)}, bf16[1024,512]{1,0:T(8,128)(2,1)}, u32[]{:S(2)}) copy-start(bf16[1024,512]{1,0:T(8,128)(2,1)} %param.6) | copy-start | bytes 3145732
  8.0 57.8 %all-gather.4.cloned.1.call-start = ((), (), s32[]{:S(2)}) async-start(), calls=%async_computation.6 | async-start | bytes 2228224 | tf_op jit(solution)/shard_map/all_gather | solution.py:14
  8.7 78.9 %reduce-scatter.5.cloned.1.call-start = ((), (), s32[]{:S(2)}) async-start(), calls=%async_computation.9 | async-start | bytes 4718592 | tf_op jit(solution)/shard_map/reduce_scatter | solution.py:39
  47.5 1.4 copy-start.1
  53.2 12.6 %copy-start.4 = (bf16[512,1024]{1,0:T(8,128)(2,1)S(1)}, bf16[512,1024]{1,0:T(8,128)(2,1)}, u32[]{:S(2)}) copy-start(bf16[512,1024]{1,0:T(8,128)(2,1)} %param.5) | copy-start | bytes 3145732
  53.3 73.2 %reduce-scatter.3.cloned.1.call-start = ((), (), s32[]{:S(2)}) async-start(), calls=%async_computation.7 | async-start | bytes 4718592 | tf_op jit(solution)/shard_map/reduce_scatter | solution.py:39
  71.8 93.5 %all-gather.6.cloned.1.call-start = ((), (), s32[]{:S(2)}) async-start(), calls=%async_computation.8 | async-start | bytes 4718592 | tf_op jit(solution)/shard_map/all_gather | solution.py:25
  131.0 68.5 %all-gather.8.cloned.1.call-start = ((), (), s32[]{:S(2)}) async-start(), calls=%async_computation.10 | async-start | bytes 4718592 | tf_op jit(solution)/shard_map/all_gather | solution.py:25
  171.1 35.9 %all-to-all-start = ((bf16[16,128,512]{2,1,0:T(8,128)(2,1)}), bf16[16,128,512]{2,1,0:T(8,128)(2,1)S(1)}, u32[]{:S(2)}, u32[]{:S(2)}) async-start(bf16[16,128,512]{2,1,0:T(8,128)(2,1)} %bitcast.24), calls=%async_computation.1 | async-start | bytes 4194304 | tf_op jit(solution)/shard_map/all_to_all | solution.py:51
  207.1 31.0 %all-to-all-start.3 = ((bf16[16,128,512]{2,1,0:T(8,128)(2,1)}), bf16[16,128,512]{2,1,0:T(8,128)(2,1)}, u32[]{:S(2)}, u32[]{:S(2)}) async-start(bf16[16,128,512]{2,1,0:T(8,128)(2,1)} %bitcast.23), calls=%async_computation.5 | async-start | bytes 4194304 | tf_op jit(solution)/shard_map/all_to_all | solution.py:51
  228.5 0.9 copy-start.3
  229.4 19.2 %copy-start.2 = (bf16[128,512]{1,0:T(8,128)(2,1)S(1)}, bf16[128,512]{1,0:T(8,128)(2,1)}, u32[]{:S(2)}) copy-start(bf16[128,512]{1,0:T(8,128)(2,1)} %param.7) | copy-start | bytes 393220
  238.1 13.9 %all-to-all-start.1 = ((bf16[8,16,512]{2,1,0:T(8,128)(2,1)}), bf16[8,16,512]{2,1,0:T(8,128)(2,1)S(1)}, u32[]{:S(2)}, u32[]{:S(2)}) async-start(bf16[8,16,512]{2,1,0:T(8,128)(2,1)} %bitcast.1), calls=%async_computation.2 | async-start | bytes 262144 | tf_op jit(solution)/shard_map/all_to_all | solution.py:64
Sparse Core Ops, SparseCore 0:
  11.0 54.8 all-gather.3
Sparse Core Ops, SparseCore 1:
  53.4 34.3 reduce-scatter.4
  89.9 36.4 reduce-scatter.2
  131.1 34.1 all-gather.5
  167.6 31.9 all-gather.7
where the time goes:
time: 261 us; the launch traced here: 260 us
  waiting for transfers between devices  136 us (52%)
  blocking collectives  37.6 us (14%)
  matrix products  35.4 us (14%)
  starting transfers between devices  20.9 us (8%)
  between operations  15.7 us (6%)
  other arithmetic  8.13 us (3%)
  local copies, waits for them, and re-layouts  6.64 us (3%)
    all_gather x2, waiting for transfers between devices, hidden_panel(): return lax.all_gather(local_rows, 'col', axis=0, tiled=True)  55.2 us
    reduce_scatter x2, waiting for transfers between devices, width_split(): lax.psum_scatter(term.astype(jnp.bfloat16), 'col', scatter_dimension=0, t...  54.6 us
    all_to_all x1, blocking collectives, token_panel_a2a(): lax.all_to_all(copies, 'row', split_axis=0, concat_axis=0, tiled=True)  37.6 us
    all_gather x1, waiting for transfers between devices, token_panel(): return lax.all_gather(local_rows, 'row', axis=0, tiled=True)  12.5 us
    all_to_all x2, starting transfers between devices, unit_sum(): lax.all_to_all(pieces, 'row', split_axis=0, concat_axis=0, tiled=True)  12.1 us
    dot_general x2, matrix products, contract_last(): lax.dot_general(left, right, (((1,), (1,)), ((), ())), preferred_element_...  10.5 us
    all_to_all x2, waiting for transfers between devices, unit_sum(): lax.all_to_all(pieces, 'row', split_axis=0, concat_axis=0, tiled=True)  9.4 us
    all_to_all x1, starting transfers between devices, local(): lax.all_to_all(block_rows, 'col', split_axis=0, concat_axis=1, tiled=True)  8.57 us
  transfers between devices with their start and end apart: 8, of which 8 were waited for; matrix products, arithmetic and copies ran while one was open for 17% of the time, Pallas kernels for 0%

commit v1 on v0

--- a/solution.py
+++ b/solution.py
@@ -22,7 +22,9 @@
 
 
 def hidden_panel(local_rows):
-    return lax.all_gather(local_rows, "col", axis=0, tiled=True)
+    return jnp.concatenate(
+        lax.all_to_all(jnp.stack([local_rows] * lax.axis_size("col")), "col", 0, 0), axis=0
+    )
 
 
 def contract_last(left, right):

time: 261 us -> 332 us (1.27)
  blocking collectives: 37.6 us -> 93.9 us
  waiting for transfers between devices: 136 us -> 143 us
  starting transfers between devices: 20.9 us -> 26.5 us
  local copies, waits for them, and re-layouts: 6.64 us -> 11 us
    all_to_all x0 -> x1, blocking collectives: none -> 56.3 us  [hidden_panel(): lax.all_to_all(jnp.stack([local_rows] * lax.axis_size('col')), 'col', 0, 0)]
    all_gather x2 -> x0, waiting for transfers between devices: 55.2 us -> none  [hidden_panel(): return lax.all_gather(local_rows, 'col', axis=0, tiled=True)]
    all_to_all x0 -> x1, waiting for transfers between devices: none -> 43.1 us  [hidden_panel(): lax.all_to_all(jnp.stack([local_rows] * lax.axis_size('col')), 'col', 0, 0)]
    all_to_all x2, waiting for transfers between devices: 9.4 us -> 27.7 us  [unit_sum(): lax.all_to_all(pieces, 'row', split_axis=0, concat_axis=0, tiled=True)]
    all_to_all x0 -> x1, starting transfers between devices: none -> 5.46 us  [hidden_panel(): lax.all_to_all(jnp.stack([local_rows] * lax.axis_size('col')), 'col', 0, 0)]
  transfers between devices with their start and end apart: 8 -> 7, of which waited for: 8 -> 7; matrix products, arithmetic and copies ran while one was open for 17% -> 13% of each run, Pallas kernels for 0% -> 0%
where the time goes in v1:
time: 332 us; the launch traced here: 331 us
  waiting for transfers between devices  143 us (43%)
  blocking collectives  93.9 us (28%)
  matrix products  35.6 us (11%)
  starting transfers between devices  26.5 us (8%)
  between operations  15.6 us (5%)
  local copies, waits for them, and re-layouts  11 us (3%)
  other arithmetic  5.76 us (2%)
    all_to_all x1, blocking collectives, hidden_panel(): lax.all_to_all(jnp.stack([local_rows] * lax.axis_size('col')), 'col', 0, 0)  56.3 us
    reduce_scatter x2, waiting for transfers between devices, width_split(): lax.psum_scatter(term.astype(jnp.bfloat16), 'col', scatter_dimension=0, t...  54.7 us
    all_to_all x1, waiting for transfers between devices, hidden_panel(): lax.all_to_all(jnp.stack([local_rows] * lax.axis_size('col')), 'col', 0, 0)  43.1 us
    all_to_all x1, blocking collectives, token_panel_a2a(): lax.all_to_all(copies, 'row', split_axis=0, concat_axis=0, tiled=True)  37.6 us
    all_to_all x2, waiting for transfers between devices, unit_sum(): lax.all_to_all(pieces, 'row', split_axis=0, concat_axis=0, tiled=True)  27.7 us
    all_gather x1, waiting for transfers between devices, token_panel(): return lax.all_gather(local_rows, 'row', axis=0, tiled=True)  12.6 us
    all_to_all x2, starting transfers between devices, unit_sum(): lax.all_to_all(pieces, 'row', split_axis=0, concat_axis=0, tiled=True)  11.9 us
    dot_general x2, matrix products, contract_last(): lax.dot_general(left, right, (((1,), (1,)), ((), ())), preferred_element_...  10.6 us
  transfers between devices with their start and end apart: 7, of which 7 were waited for; matrix products, arithmetic and copies ran while one was open for 13% of the time, Pallas kernels for 0%

profile of v1, /device:TPU:1, one launch (start us, length us, event | category | flops | bytes accessed | tf_op | source)
XLA Modules:
  0.0 331.3 jit_solution(14182442566494808253)
XLA Ops:
  8.1 0.7 all-gather.2.cloned.1.call-update
  8.8 1.1 broadcast_in_dim.2
  9.9 37.6 %all_to_all.48 = bf16[16,128,512]{2,1,0:T(8,128)(2,1)S(1)} all-to-all(bf16[16,128,512]{2,1,0:T(8,128)(2,1)S(1)} %broadcast_in_dim.2), channel_id=1, replica_groups=mesh['row'=16,'col'=8] {'row'}, dimensions={0} | all-to-all | bytes 4194304 | tf_op jit(solution)/shard_map/all_to_all | solution.py:21
  47.5 1.3 copy-done.3
  48.9 4.3 %convolution_convert_fusion = bf16[2048,1024]{1,0:T(8,128)(2,1)} fusion(bf16[2048,512]{1,0:T(8,128)(2,1)S(1)} %bitcast.25, bf16[1024,512]{1,0:T(8,128)(2,1)S(1)} %copy-done), kind=kOutput, calls=%fused_computation.2 | convolution fusion | flops 2149580800 | bytes 7340032 | tf_op jit(solution)/shard_map/dot_general | solution.py:31
  53.3 12.6 %all-gather.2.cloned.1.call-done = bf16[2048,512]{1,0:T(8,128)(2,1)} async-done(((bf16[128,512]{1,0:T(8,128)(2,1)}), bf16[2048,512]{1,0:T(8,128)(2,1)}) %all-gather.2.cloned.1.call-update) | async-done | bytes 2097168 | tf_op jit(solution)/shard_map/all_gather | solution.py:14
  65.8 6.0 %convolution_convert_fusion.1 = bf16[2048,1024]{1,0:T(8,128)(2,1)} fusion(bf16[2048,512]{1,0:T(8,128)(2,1)} %all-gather.2.cloned.1.call-done, bf16[512,1024]{1,0:T(8,128)(2,1)S(1)} %copy-done.6), kind=kOutput, calls=%fused_computation.3 | convolution fusion | flops 2149580800 | bytes 7340032 | tf_op jit(solution)/shard_map/dot_general | solution.py:40
  71.8 15.8 %reduce-scatter.5.cloned.1.call-done = bf16[256,1024]{1,0:T(8,128)(2,1)} async-done(((bf16[2048,1024]{1,0:T(8,128)(2,1)}), bf16[256,1024]{1,0:T(8,128)(2,1)}) %reduce-scatter.5.cloned.1.call-update) | async-done | bytes 524304 | tf_op jit(solution)/shard_map/reduce_scatter | solution.py:41
  87.6 38.9 %reduce-scatter.3.cloned.1.call-done = bf16[256,1024]{1,0:T(8,128)(2,1)} async-done(((bf16[2048,1024]{1,0:T(8,128)(2,1)}), bf16[256,1024]{1,0:T(8,128)(2,1)}) %reduce-scatter.3.cloned.1.call-update) | async-done | bytes 524304 | tf_op jit(solution)/shard_map/reduce_scatter | solution.py:41
  126.5 3.8 %fusion.38 = (bf16[256,1024]{1,0:T(8,128)(2,1)S(1)}, bf16[256,1024]{1,0:T(8,128)(2,1)S(1)}) fusion(bf16[256,1024]{1,0:T(8,128)(2,1)} %reduce-scatter.3.cloned.1.call-done, bf16[256,1024]{1,0:T(8,128)(2,1)} %reduce-scatter.5.cloned.1.call-done), kind=kLoop, calls=%fused_computation.52 | loop fusion | flops 20185088 | bytes 2097152 | tf_op jit(solution)/shard_map/convert_element_type | solution.py:63
  130.3 0.5 stack.4
  130.8 56.3 %all_to_all.49 = bf16[8,256,1024]{2,1,0:T(8,128)(2,1)} all-to-all(bf16[8,256,1024]{2,1,0:T(8,128)(2,1)S(1)} %stack.4), channel_id=1, replica_groups=mesh['row'=16,'col'=8] {'col'}, dimensions={0} | all-to-all | bytes 8388608 | tf_op jit(solution)/shard_map/all_to_all | solution.py:26
  187.1 2.5 stack.5
  189.6 5.5 %all-to-all-start.4 = ((bf16[8,256,1024]{2,1,0:T(8,128)(2,1)}), bf16[8,256,1024]{2,1,0:T(8,128)(2,1)}, u32[]{:S(2)}, u32[]{:S(2)}) async-start(bf16[8,256,1024]{2,1,0:T(8,128)(2,1)} %stack.5), calls=%async_computation.6 | async-start | bytes 8388608 | tf_op jit(solution)/shard_map/all_to_all | solution.py:26
  195.1 5.8 %convolution_convert_fusion.3 = bf16[2048,512]{1,0:T(8,128)(2,1)} fusion(bf16[2048,1024]{1,0:T(8,128)(2,1)} %bitcast.23, bf16[1024,512]{1,0:T(8,128)(2,1)S(1)} %copy-done), kind=kOutput, calls=%fused_computation.5 | convolution fusion | flops 2148532224 | bytes 7340032 | tf_op jit(solution)/shard_map/dot_general | solution.py:51
  200.9 43.1 %all-to-all-done.4 = bf16[8,256,1024]{2,1,0:T(8,128)(2,1)} async-done(((bf16[8,256,1024]{2,1,0:T(8,128)(2,1)}), bf16[8,256,1024]{2,1,0:T(8,128)(2,1)}, u32[]{:S(2)}, u32[]{:S(2)}) %all-to-all-start.4) | async-done | bytes 4194336 | tf_op jit(solution)/shard_map/all_to_all | solution.py:26
  244.0 6.6 %all-to-all-start.1 = ((bf16[16,128,512]{2,1,0:T(8,128)(2,1)}), bf16[16,128,512]{2,1,0:T(8,128)(2,1)S(1)}, u32[]{:S(2)}, u32[]{:S(2)}) async-start(bf16[16,128,512]{2,1,0:T(8,128)(2,1)} %bitcast.28), calls=%async_computation.2 | async-start | bytes 4194304 | tf_op jit(solution)/shard_map/all_to_all | solution.py:53
  250.6 6.2 %convolution_convert_fusion.2 = bf16[2048,512]{1,0:T(8,128)(2,1)} fusion(bf16[2048,1024]{1,0:T(8,128)(2,1)} %bitcast.5, bf16[512,1024]{1,0:T(8,128)(2,1)} %param.5), kind=kOutput, calls=%fused_computation.4 | convolution fusion | flops 2148532224 | bytes 7340032 | tf_op jit(solution)/shard_map/dot_general | solution.py:31
  256.8 20.2 %all-to-all-done.1 = bf16[16,128,512]{2,1,0:T(8,128)(2,1)S(1)} async-done(((bf16[16,128,512]{2,1,0:T(8,128)(2,1)}), bf16[16,128,512]{2,1,0:T(8,128)(2,1)S(1)}, u32[]{:S(2)}, u32[]{:S(2)}) %all-to-all-start.1) | async-done | bytes 2097184 | tf_op jit(solution)/shard_map/all_to_all | solution.py:53
  277.1 1.3 copy-done.1
  278.4 5.3 %all-to-all-start.5 = ((bf16[16,128,512]{2,1,0:T(8,128)(2,1)}), bf16[16,128,512]{2,1,0:T(8,128)(2,1)S(1)}, u32[]{:S(2)}, u32[]{:S(2)}) async-start(bf16[16,128,512]{2,1,0:T(8,128)(2,1)} %bitcast.27), calls=%async_computation.7 | async-start | bytes 4194304 | tf_op jit(solution)/shard_map/all_to_all | solution.py:53
  283.7 6.5 %convolution_bitcast_fusion = f32[512,1024]{0,1:T(8,128)} fusion(bf16[2048,1024]{1,0:T(8,128)(2,1)} %bitcast.5, bf16[2048,512]{1,0:T(8,128)(2,1)} %all-gather.2.cloned.1.call-done), kind=kOutput, calls=%fused_computation.12 | convolution fusion | flops 2147483648 | bytes 8388608 | tf_op jit(solution)/shard_map/dot_general | solution.py:70
  290.2 2.9 copy.12
  293.1 6.7 %fusion.39 = f32[1024,512]{1,0:T(8,128)} fusion(bf16[2048,1024]{1,0:T(8,128)(2,1)} %bitcast.24, bf16[2048,512]{1,0:T(8,128)(2,1)} %bitcast.26), kind=kOutput, calls=%fused_computation.55 | convolution fusion | flops 2147483648 | bytes 8388608 | tf_op jit(solution)/shard_map/dot_general | solution.py:67
  299.8 0.3 convert_reduce_fusion.1
  300.1 0.6 copy-done.5
  300.7 0.7 add_convert_fusion.1
  301.4 7.5 %all-to-all-done.5 = bf16[16,128,512]{2,1,0:T(8,128)(2,1)S(1)} async-done(((bf16[16,128,512]{2,1,0:T(8,128)(2,1)}), bf16[16,128,512]{2,1,0:T(8,128)(2,1)S(1)}, u32[]{:S(2)}, u32[]{:S(2)}) %all-to-all-start.5) | async-done | bytes 2097184 | tf_op jit(solution)/shard_map/all_to_all | solution.py:53
  308.8 9.1 %all-to-all-start.2 = ((bf16[8,16,512]{2,1,0:T(8,128)(2,1)}), bf16[8,16,512]{2,1,0:T(8,128)(2,1)S(1)}, u32[]{:S(2)}, u32[]{:S(2)}) async-start(bf16[8,16,512]{2,1,0:T(8,128)(2,1)} %bitcast.2), calls=%async_computation.3 | async-start | bytes 262144 | tf_op jit(solution)/shard_map/all_to_all | solution.py:66
  318.2 0.7 add_convert_fusion
  318.9 4.3 %all-to-all-done.2 = bf16[8,16,512]{2,1,0:T(8,128)(2,1)S(1)} async-done(((bf16[8,16,512]{2,1,0:T(8,128)(2,1)}), bf16[8,16,512]{2,1,0:T(8,128)(2,1)S(1)}, u32[]{:S(2)}, u32[]{:S(2)}) %all-to-all-start.2) | async-done | bytes 131104 | tf_op jit(solution)/shard_map/all_to_all | solution.py:66
  323.2 0.7 copy.13
  (17 shorter events, 0.5 us)
Async XLA Ops:
  8.0 40.9 %copy-start = (bf16[1024,512]{1,0:T(8,128)(2,1)S(1)}, bf16[1024,512]{1,0:T(8,128)(2,1)}, u32[]{:S(2)}) copy-start(bf16[1024,512]{1,0:T(8,128)(2,1)} %param.6) | copy-start | bytes 3145732
  8.0 57.8 %all-gather.2.cloned.1.call-start = ((), (), s32[]{:S(2)}) async-start(), calls=%async_computation.8 | async-start | bytes 2228224 | tf_op jit(solution)/shard_map/all_gather | solution.py:14
  8.7 78.9 %reduce-scatter.5.cloned.1.call-start = ((), (), s32[]{:S(2)}) async-start(), calls=%async_computation.10 | async-start | bytes 4718592 | tf_op jit(solution)/shard_map/reduce_scatter | solution.py:41
  47.5 1.3 copy-start.3
  53.2 12.6 %copy-start.6 = (bf16[512,1024]{1,0:T(8,128)(2,1)S(1)}, bf16[512,1024]{1,0:T(8,128)(2,1)}, u32[]{:S(2)}) copy-start(bf16[512,1024]{1,0:T(8,128)(2,1)} %param.5) | copy-start | bytes 3145732
  53.2 73.2 %reduce-scatter.3.cloned.1.call-start = ((), (), s32[]{:S(2)}) async-start(), calls=%async_computation.9 | async-start | bytes 4718592 | tf_op jit(solution)/shard_map/reduce_scatter | solution.py:41
  189.6 54.4 %all-to-all-start.4 = ((bf16[8,256,1024]{2,1,0:T(8,128)(2,1)}), bf16[8,256,1024]{2,1,0:T(8,128)(2,1)}, u32[]{:S(2)}, u32[]{:S(2)}) async-start(bf16[8,256,1024]{2,1,0:T(8,128)(2,1)} %stack.5), calls=%async_computation.6 | async-start | bytes 8388608 | tf_op jit(solution)/shard_map/all_to_all | solution.py:26
  244.0 33.1 %all-to-all-start.1 = ((bf16[16,128,512]{2,1,0:T(8,128)(2,1)}), bf16[16,128,512]{2,1,0:T(8,128)(2,1)S(1)}, u32[]{:S(2)}, u32[]{:S(2)}) async-start(bf16[16,128,512]{2,1,0:T(8,128)(2,1)} %bitcast.28), calls=%async_computation.2 | async-start | bytes 4194304 | tf_op jit(solution)/shard_map/all_to_all | solution.py:53
  277.0 1.3 copy-start.1
  278.4 30.4 %all-to-all-start.5 = ((bf16[16,128,512]{2,1,0:T(8,128)(2,1)}), bf16[16,128,512]{2,1,0:T(8,128)(2,1)S(1)}, u32[]{:S(2)}, u32[]{:S(2)}) async-start(bf16[16,128,512]{2,1,0:T(8,128)(2,1)} %bitcast.27), calls=%async_computation.7 | async-start | bytes 4194304 | tf_op jit(solution)/shard_map/all_to_all | solution.py:53
  293.1 6.7 %copy-start.2 = (bf16[16,128,512]{2,1,0:T(8,128)(2,1)S(1)}, bf16[16,128,512]{2,1,0:T(8,128)(2,1)}, u32[]{:S(2)}) copy-start(bf16[16,128,512]{2,1,0:T(8,128)(2,1)} %copy-done.1) | copy-start | bytes 6291460
  299.8 0.9 copy-start.5
  300.7 17.5 %copy-start.4 = (bf16[128,512]{1,0:T(8,128)(2,1)S(1)}, bf16[128,512]{1,0:T(8,128)(2,1)}, u32[]{:S(2)}) copy-start(bf16[128,512]{1,0:T(8,128)(2,1)} %param.7) | copy-start | bytes 393220
  308.8 14.4 %all-to-all-start.2 = ((bf16[8,16,512]{2,1,0:T(8,128)(2,1)}), bf16[8,16,512]{2,1,0:T(8,128)(2,1)S(1)}, u32[]{:S(2)}, u32[]{:S(2)}) async-start(bf16[8,16,512]{2,1,0:T(8,128)(2,1)} %bitcast.2), calls=%async_computation.3 | async-start | bytes 262144 | tf_op jit(solution)/shard_map/all_to_all | solution.py:66
Sparse Core Ops, SparseCore 0:
  11.0 54.8 all-gather.1
Sparse Core Ops, SparseCore 1:
  53.3 34.3 reduce-scatter.4
  89.9 36.5 reduce-scatter.2
